TPU v7x, 256 devices: a whole 4x4x8 slice. The times are simulated.
256 devices in a mesh: dp: 2 (over z_lo), seq: 32 (over y, x, core), head: 4 (over z_hi).
Axes of the slice: x: 4, y: 4, z: 8 (z_hi: 4, z_lo: 2; z = z_hi * 2 + z_lo), core: 2. Of those that a mesh axis runs over, the one named last changes fastest.
Arguments:
- query_rows: bfloat16 [2, 8192, 4096], P('dp', 'seq', 'head'), may hold values from -0.59765625 to 0.59765625
- key_rows: bfloat16 [2, 8192, 4096], P('dp', 'seq', 'head'), may hold values from -0.59765625 to 0.59765625
- value_rows: bfloat16 [2, 8192, 4096], P('dp', 'seq', 'head'), may hold values from -1536 to 1536
- grad_out: bfloat16 [2, 8192, 6144], P('dp', 'seq'), may hold values from -6 to 6
- out_weight: bfloat16 [6144, 4096], P('seq', 'head'), may hold values from -0.09375 to 0.09375
- decay_rates: float32 [32], P('head'), may hold values from 0 to 1, as said below
- doc_blocks: int32 [2, 64], P('dp'), may hold values from 0 to 7, never falling along the last dimension, each value on 1 to 32 neighbouring positions
Outputs:
- grad_query: bfloat16 [2, 8192, 4096], P('dp', 'seq', 'head')
- grad_key: bfloat16 [2, 8192, 4096], P('dp', 'seq', 'head')
- grad_value: bfloat16 [2, 8192, 4096], P('dp', 'seq', 'head')
- grad_weight: float32 [6144, 4096], P('seq', 'head')
Inputs may be any that keep to these rules, and one draw needn't show every extreme that they name: `doc_blocks`: in each pack document numbers never fall from block to block; every document covers 1 to 32 blocks, and one covers exactly 32. `decay_rates`: rates are positive.
All inputs are finite; a program needn't handle non-finite values.
Results may differ from a plain program's by a relative error of at most 0.024.
Values may be sent and summed in bfloat16 or wider, within the bound.
No kernel may reach another device: no remote copies, remote signals or barrier semaphores. Data moves between devices by JAX's collectives and lax.ppermute only.
A program may use at most 192 MiB of HBM per device.

v0:
```python
import jax
import jax.numpy as jnp
from jax import lax
from jax.sharding import PartitionSpec as P

BLOCK = 128
EPSILON = 1e-05


def prefix(array, axis, join, neutral, backward):
    count = lax.axis_size(axis)
    place = lax.axis_index(axis)
    ahead = count - 1 - place if backward else place
    gathered = jax.tree.map(
        lambda a, kind: lax.all_gather(a.astype(kind), axis), array, (jnp.bfloat16, jnp.bfloat16)
    )
    state = jax.tree.map(lambda a, e: jnp.zeros_like(a) + jnp.asarray(e, a.dtype), array, neutral)

    def one(step, state):
        source = count - 1 - step if backward else step
        return join(
            state,
            jax.tree.map(
                lambda a, own: lax.dynamic_index_in_dim(a, source, 0, False).astype(own.dtype),
                gathered,
                array,
            ),
        )

    return lax.fori_loop(0, ahead, one, state)


def block_docs(doc_row, first_block, block_count, block_len):
    blocks = lax.dynamic_slice_in_dim(doc_row, first_block, block_count)
    return jnp.reshape(
        jnp.broadcast_to(blocks[:, None], (block_count, block_len)), (block_count * block_len,)
    )


def decay_masks(token_docs, decay_rates, prev_doc, next_doc):
    length = token_docs.shape[0]
    position = jnp.arange(length).astype(jnp.float32)
    rates = decay_rates[:, None]
    distance = position[:, None] - position[None, :]
    allowed = jnp.logical_and(distance >= 0, token_docs[:, None] == token_docs[None, :])
    intra = jnp.where(
        allowed[None], jnp.exp(-rates[:, :, None] * jnp.maximum(distance, 0.0)[None]), 0.0
    )
    weight_end = jnp.where(
        (token_docs == token_docs[length - 1])[None],
        jnp.exp(-rates * (length - 1.0 - position)[None]),
        0.0,
    )
    weight_start = jnp.where(
        (token_docs == token_docs[0])[None], jnp.exp(-rates * position[None]), 0.0
    )
    weight_before = jnp.where(
        (token_docs == prev_doc)[None], jnp.exp(-rates * (position + 1.0)[None]), 0.0
    )
    weight_after = jnp.where(
        (token_docs == next_doc)[None], jnp.exp(-rates * (length - position)[None]), 0.0
    )
    span_decay = jnp.exp(-decay_rates * float(length))
    link_fwd = jnp.where(token_docs[length - 1] == prev_doc, span_decay, 0.0)
    link_rev = jnp.where(token_docs[0] == next_doc, span_decay, 0.0)
    return (intra, weight_end, weight_start, weight_before, weight_after, link_fwd, link_rev)


def combine_states(earlier, later):
    return (earlier[0] * later[0], later[0][:, None, None] * earlier[1] + later[1])


def local_state(keys_here, values_here, weight_end):
    weighted = (keys_here.astype(jnp.float32) * weight_end.T[:, :, None]).astype(jnp.bfloat16)
    return jnp.einsum("jhd,jhe->hde", weighted, values_here, preferred_element_type=jnp.float32)


def forward_out(queries, keys_here, values_here, intra, weight_before, state_in):
    scores = jnp.einsum("thd,jhd->htj", queries, keys_here, preferred_element_type=jnp.float32)
    attention = (scores * intra).astype(jnp.bfloat16)
    state_low = state_in.astype(jnp.bfloat16)
    carried = jnp.einsum("thd,hde->the", queries, state_low, preferred_element_type=jnp.float32)
    output = (
        jnp.einsum("htj,jhe->the", attention, values_here, preferred_element_type=jnp.float32)
        + weight_before.T[:, :, None] * carried
    )
    inverse_rms = lax.rsqrt(jnp.mean(output * output, axis=-1, keepdims=True) + EPSILON)
    return (attention, state_low, output * inverse_rms, inverse_rms)


def backward_local(queries, values_here, intra, normal, inverse_rms, grad_normed, weight_start):
    inner = jnp.mean(grad_normed * normal, axis=-1, keepdims=True)
    grad_attn = (inverse_rms * (grad_normed - normal * inner)).astype(jnp.bfloat16)
    grad_scores = (
        jnp.einsum("the,jhe->htj", grad_attn, values_here, preferred_element_type=jnp.float32)
        * intra
    ).astype(jnp.bfloat16)
    weighted = (queries.astype(jnp.float32) * weight_start.T[:, :, None]).astype(jnp.bfloat16)
    back_local = jnp.einsum("thd,the->hde", weighted, grad_attn, preferred_element_type=jnp.float32)
    return (grad_attn, grad_scores, back_local)


def backward_rest(
    queries,
    keys_here,
    values_here,
    attention,
    state_low,
    grad_attn,
    grad_scores,
    weight_before,
    weight_after,
    state_back,
):
    back_low = state_back.astype(jnp.bfloat16)
    grad_query = jnp.einsum(
        "htj,jhd->thd", grad_scores, keys_here, preferred_element_type=jnp.float32
    ) + weight_before.T[:, :, None] * jnp.einsum(
        "the,hde->thd", grad_attn, state_low, preferred_element_type=jnp.float32
    )
    grad_key = jnp.einsum(
        "htj,thd->jhd", grad_scores, queries, preferred_element_type=jnp.float32
    ) + weight_after.T[:, :, None] * jnp.einsum(
        "jhe,hde->jhd", values_here, back_low, preferred_element_type=jnp.float32
    )
    grad_value = jnp.einsum(
        "htj,the->jhe", attention, grad_attn, preferred_element_type=jnp.float32
    ) + weight_after.T[:, :, None] * jnp.einsum(
        "jhd,hde->jhe", keys_here, back_low, preferred_element_type=jnp.float32
    )
    return (
        grad_query.astype(jnp.bfloat16),
        grad_key.astype(jnp.bfloat16),
        grad_value.astype(jnp.bfloat16),
    )


def local(query_rows, key_rows, value_rows, grad_out, out_weight, decay_rates, doc_blocks):
    tok_count = query_rows.shape[1]
    heads_here = decay_rates.shape[0]
    head_dim = query_rows.shape[2] // heads_here
    seq_count = lax.axis_size("seq")
    span_index = lax.axis_index("seq")
    block_count = tok_count // BLOCK
    total_blocks = doc_blocks.shape[1]
    queries = query_rows[0].reshape(tok_count, heads_here, head_dim)
    keys_here = key_rows[0].reshape(tok_count, heads_here, head_dim)
    values_here = value_rows[0].reshape(tok_count, heads_here, head_dim)
    grad_rows = grad_out[0]
    doc_row = doc_blocks[0]
    first_block = span_index * block_count
    token_docs = block_docs(doc_row, first_block, block_count, BLOCK)
    prev_doc = doc_row[jnp.maximum(first_block - 1, 0)]
    next_doc = doc_row[jnp.minimum(first_block + block_count, total_blocks - 1)]
    intra, weight_end, weight_start, weight_before, weight_after, link_fwd, link_rev = decay_masks(
        token_docs, decay_rates, prev_doc, next_doc
    )
    state_local = local_state(keys_here, values_here, weight_end)
    identity = (jnp.ones_like(link_fwd), jnp.zeros_like(state_local))
    state_in = prefix((link_fwd, state_local), "seq", combine_states, identity, False)[1]
    attention, state_low, normal, inverse_rms = forward_out(
        queries, keys_here, values_here, intra, weight_before, state_in
    )
    columns = grad_rows
    grad_normed = jnp.dot(
        columns,
        lax.all_gather(out_weight, "seq", axis=0, tiled=True),
        preferred_element_type=jnp.float32,
    )
    normed = normal.astype(jnp.bfloat16).reshape(tok_count, heads_here * head_dim)
    columns = grad_rows
    part = lax.dot_general(
        columns, normed, (((0,), (0,)), ((), ())), preferred_element_type=jnp.float32
    )
    weight_part = lax.psum_scatter(
        part.astype(jnp.bfloat16).astype(jnp.float32).astype(jnp.bfloat16),
        "seq",
        scatter_dimension=0,
        tiled=True,
    )
    norm_factor = (lax.axis_size("dp") * seq_count * tok_count) ** (-0.5)
    grad_weight = lax.psum(weight_part, "dp").astype(jnp.float32) * norm_factor
    grad_attn, grad_scores, back_local = backward_local(
        queries,
        values_here,
        intra,
        normal,
        inverse_rms,
        grad_normed.reshape(tok_count, heads_here, head_dim),
        weight_start,
    )
    back_identity = (jnp.ones_like(link_rev), jnp.zeros_like(back_local))
    state_back = prefix((link_rev, back_local), "seq", combine_states, back_identity, True)[1]
    grad_query, grad_key, grad_value = backward_rest(
        queries,
        keys_here,
        values_here,
        attention,
        state_low,
        grad_attn,
        grad_scores,
        weight_before,
        weight_after,
        state_back,
    )
    flat_shape = (1, tok_count, heads_here * head_dim)
    return (
        grad_query.reshape(flat_shape),
        grad_key.reshape(flat_shape),
        grad_value.reshape(flat_shape),
        grad_weight,
    )


def solution(mesh):
    in_specs = (
        P("dp", "seq", "head"),
        P("dp", "seq", "head"),
        P("dp", "seq", "head"),
        P("dp", "seq", None),
        P("seq", "head"),
        P("head"),
        P("dp", None),
    )
    out_specs = (
        P("dp", "seq", "head"),
        P("dp", "seq", "head"),
        P("dp", "seq", "head"),
        P("seq", "head"),
    )
    return jax.shard_map(local, mesh=mesh, in_specs=in_specs, out_specs=out_specs, check_vma=False)
```

profile of v0, /device:TPU:1, one launch (start us, length us, event | category | flops | bytes accessed | tf_op | source)
XLA Modules:
  0.0 419.0 jit_solution(4983138501228653416)
XLA Ops:
  8.8 1.3 constant_dynamic-slice_fusion
  12.7 2.7 bitcast_compare_fusion.3
  15.4 1.9 copy.85
  17.3 2.1 copy.58
  19.5 1.1 copy.86
  21.4 2.0 convolution_convert_fusion.1
  26.0 66.1 %all-reduce.2 = (bf16[256]{0:T(256)(128)(2,1)S(1)}, bf16[256]{0:T(256)(128)(2,1)S(1)}) all-reduce(bf16[256]{0:T(256)(128)(2,1)S(1)} %dynamic-update-slice, bf16[256]{0:T(256)(128)(2,1)S(1)} %dynamic-update-slice.1), channel_id=2, replica_groups=mesh['dp'=2,'seq'=32,'head'=4] {'seq'}, use_global_device_ids=true, to_apply=%add | all-reduce | flops 512 | bytes 2048
  92.1 2.1 copy.84
  94.4 1.9 multiply_convert_fusion.1
  97.3 1.5 convolution_bitcast_fusion.7
  99.7 2.1 while.26
  99.7 2.1 convert_add_fusion.4
  101.8 3.0 multiply_reduce_fusion.1
  104.7 51.4 %all-gather.8.cloned.1.call-done = bf16[6144,1024]{1,0:T(8,128)(2,1)} async-done(((bf16[192,1024]{1,0:T(8,128)(2,1)}), bf16[6144,1024]{1,0:T(8,128)(2,1)}) %all-gather.8.cloned.1.call-update) | async-done | bytes 12582928 | tf_op jit(solution)/shard_map/all_gather | solution.py:167
  156.1 16.7 %copy.62 = bf16[1024,6144]{1,0:T(8,128)(2,1)} copy(bf16[1024,6144]{0,1:T(8,128)(2,1)} %bitcast.111) | data formatting | bytes 25165824 | tf_op jit(solution)/shard_map/dot_general | solution.py:165
  172.8 7.0 %multiply_reduce_fusion = (f32[256,8]{0,1:T(8,128)S(1)}, f32[256,8,128]{0,2,1:T(8,128)S(1)}) fusion(f32[256,8,128]{0,2,1:T(8,128)} %get-tuple-element.186, f32[256,8]{0,1:T(8,128)S(1)} %add_rsqrt_fusion, bf16[8,128,6144]{2,1,0:T(8,128)(2,1)} %bitcast.112, bf16[1,256,6144]{2,1,0:T(8,128)(2,1)S(1)} %copy-done), kind=kOutput, calls=%fused_computation.35 | convolution fusion | flops 3222009856 | bytes 17842176 | tf_op jit(solution)/shard_map/dot_general | solution.py:165
  182.8 7.4 %convert_bitcast_fusion = bf16[6144,1024]{0,1:T(8,128)(2,1)} fusion(bf16[256,1024]{0,1:T(8,128)(2,1)} %bitcast.127, bf16[1,256,6144]{2,1,0:T(8,128)(2,1)S(1)} %copy-done), kind=kOutput, calls=%fused_computation.4 | convolution fusion | flops 3227516928 | bytes 16252928 | tf_op jit(solution)/shard_map/dot_general | solution.py:172
  190.2 16.7 %copy.82 = bf16[6144,1024]{1,0:T(8,128)(2,1)} copy(bf16[6144,1024]{0,1:T(8,128)(2,1)} %convert_bitcast_fusion) | data formatting | bytes 25165824
  210.8 1.3 convolution_bitcast_fusion.5
  212.1 1.3 convolution_bitcast_fusion.4
  213.4 37.4 %all-gather.12.cloned.1.call-done = bf16[256,128,128]{2,1,0:T(8,128)(2,1)} async-done(((bf16[8,128,128]{2,1,0:T(8,128)(2,1)}), bf16[256,128,128]{2,1,0:T(8,128)(2,1)}) %all-gather.12.cloned.1.call-update) | async-done | bytes 8388624 | tf_op jit(solution)/shard_map/all_gather | solution.py:15
  250.9 35.0 %while.27 = (s32[]{:T(128)}, f32[8,128,128]{2,1,0:T(8,128)S(1)}, s32[]{:T(128)}, bf16[32,8]{1,0:T(8,128)(2,1)S(1)}, bf16[32,8,128,128]{3,2,1,0:T(8,128)(2,1)}, /*index=5*/s32[]{:T(128)}, s32[]{:T(128)}, s32[]{:T(128)}, s32[]{:T(128)}) while((s32[]{:T(128)}, f32[8,128,128]{2,1,0:T(8,128)S(1)}, s32[]{:T(128)}, bf16[32,8]{1,0:T(8,128)(2,1)S(1)}, ...), condition=%wide.region_5.6_spmd, body=%wide.region_4.5_spmd.sunk | while | flops 393230 | bytes 1310955 | solution.py:30
  250.9 1.2 convert_add_fusion.5
  267.1 1.1 convert_add_fusion.5
  268.3 1.1 convert_add_fusion.5
  269.5 1.1 convert_add_fusion.5
  270.6 1.1 convert_add_fusion.5
  271.8 1.1 convert_add_fusion.5
  273.0 1.2 convert_add_fusion.5
  274.2 1.1 convert_add_fusion.5
  275.3 1.1 convert_add_fusion.5
  276.5 1.2 convert_add_fusion.5
  277.7 1.1 convert_add_fusion.5
  278.9 1.1 convert_add_fusion.5
  280.0 1.1 convert_add_fusion.5
  281.2 1.1 convert_add_fusion.5
  282.4 1.1 convert_add_fusion.5
  283.5 1.1 convert_add_fusion.5
  284.7 1.2 convert_add_fusion.5
  285.9 79.1 %reduce-scatter.4.cloned.1.call-done = bf16[192,1024]{1,0:T(8,128)(2,1)} async-done(((bf16[6144,1024]{1,0:T(8,128)(2,1)}), bf16[192,1024]{1,0:T(8,128)(2,1)}) %reduce-scatter.4.cloned.1.call-update) | async-done | bytes 393232
  364.9 2.0 copy.83
  367.0 1.1 fusion.13
  368.1 2.2 copy.75
  370.3 2.7 fusion.12
  373.0 2.0 copy.74
  375.0 32.9 %all-reduce.5.cloned.1.call-done = bf16[192,1024]{0,1:T(8,128)(2,1)} async-done(((bf16[192,1024]{0,1:T(8,128)(2,1)}), bf16[192,1024]{0,1:T(8,128)(2,1)}) %all-reduce.5.cloned.1.call-update) | async-done | bytes 393232 | tf_op jit(solution)/shard_map/psum | solution.py:182
  408.0 2.1 convert_multiply_fusion
  410.0 2.4 copy.76
  (124 shorter events, 28.0 us)
Async XLA Ops:
  7.2 165.6 %copy-start = (bf16[1,256,6144]{2,1,0:T(8,128)(2,1)S(1)}, bf16[1,256,6144]{2,1,0:T(8,128)(2,1)}, u32[]{:S(2)}) copy-start(bf16[1,256,6144]{2,1,0:T(8,128)(2,1)} %param.14) | copy-start | bytes 9437188
  7.2 17.1 %copy-start.20 = (u32[256]{0:T(256)S(1)}, u32[256]{0:T(256)}, u32[]{:S(2)}) copy-start(u32[256]{0:T(256)} %constant.96) | copy-start | bytes 3076
  7.2 13.4 %copy-start.19 = (f32[8]{0:T(128)S(1)}, f32[8]{0:T(128)}, u32[]{:S(2)}) copy-start(f32[8]{0:T(128)} %param.16) | copy-start | bytes 100
  7.2 91.6 %all-gather.10.cloned.1.call-start = ((), (), s32[]{:S(2)}) async-start(), calls=%async_computation.3 | async-start | bytes 8650752 | tf_op jit(solution)/shard_map/all_gather | solution.py:15
  20.6 0.8 copy-start.8
  23.5 132.6 %all-gather.8.cloned.1.call-start = ((), (), s32[]{:S(2)}) async-start(), calls=%async_computation.1 | async-start | bytes 12976128 | tf_op jit(solution)/shard_map/all_gather | solution.py:167
  24.2 226.6 %all-gather.12.cloned.1.call-start = ((), (), s32[]{:S(2)}) async-start(), calls=%async_computation.4 | async-start | bytes 8650752 | tf_op jit(solution)/shard_map/all_gather | solution.py:15
  94.2 3.1 copy-start.9
  96.3 1.0 copy-start.13
  172.8 7.0 %copy-start.12 = (f32[256,8,128]{0,2,1:T(8,128)S(1)}, f32[256,8,128]{0,2,1:T(8,128)}, u32[]{:S(2)}) copy-start(f32[256,8,128]{0,2,1:T(8,128)} %get-tuple-element.186) | copy-start | bytes 3145732
  179.8 1.9 copy-start.6
  180.9 0.8 copy-start.4
  182.7 182.2 %reduce-scatter.4.cloned.1.call-start = ((), (), s32[]{:S(2)}) async-start(), calls=%async_computation.5 | async-start | bytes 12976128
  206.9 1.0 copy-start.5
  206.9 1.2 copy-start.10
  206.9 1.9 copy-start.18
  207.0 201.0 %all-reduce.5.cloned.1.call-start = ((), (), s32[]{:S(2)}) async-start(), calls=%async_computation.2 | async-start | bytes 1048576 | tf_op jit(solution)/shard_map/psum | solution.py:182
  208.1 1.2 copy-start.3
  208.8 1.0 copy-start.16
  208.8 2.0 copy-start.14
  209.3 2.8 copy-start.7
  210.8 1.3 copy-start.17
  250.9 116.1 %copy-start.11 = (bf16[32,8,8,128]{3,2,1,0:T(8,128)(2,1)S(1)}, bf16[32,8,8,128]{3,2,1,0:T(8,128)(2,1)}, u32[]{:S(2)}) copy-start(bf16[32,8,8,128]{3,2,1,0:T(8,128)(2,1)} %copy.85) | copy-start | bytes 1572868
  250.9 116.1 %copy-start.15 = (f32[256,8,128]{0,2,1:T(8,128)S(1)}, f32[256,8,128]{0,2,1:T(8,128)}, u32[]{:S(2)}) copy-start(f32[256,8,128]{0,2,1:T(8,128)} %convolution_bitcast_fusion.5) | copy-start | bytes 3145732
  285.9 81.1 %copy-start.2 = (f32[8,128,128]{2,1,0:T(8,128)}, f32[8,128,128]{2,1,0:T(8,128)S(1)}, u32[]{:S(2)}) copy-start(f32[8,128,128]{2,1,0:T(8,128)S(1)} %get-tuple-element.133) | copy-start | bytes 1572868
  368.1 44.3 %copy-start.1 = (bf16[1,256,6144]{2,1,0:T(8,128)(2,1)S(1)}, bf16[1,256,6144]{2,1,0:T(8,128)(2,1)}, u32[]{:S(2)}) copy-start(bf16[1,256,6144]{2,1,0:T(8,128)(2,1)} %param.14) | copy-start | bytes 9437188
Sparse Core Ops, SparseCore 0:
  23.6 62.5 all-gather.9
  88.7 67.3 all-gather.7
  182.9 67.9 all-gather.11
  254.8 110.0 reduce-scatter.3
  367.6 40.3 all-reduce.4
where the time goes:
time: 422 us; the launch traced here: 419 us
  waiting for transfers between devices  201 us (48%)
  blocking collectives  66.1 us (16%)
  local copies, waits for them, and re-layouts  59 us (14%)
  other arithmetic  42.3 us (10%)
  matrix products  31.7 us (8%)
  between operations  17.3 us (4%)
    unnamed x6, waiting for transfers between devices  79.8 us
    unnamed x1, blocking collectives  66.1 us
    all_gather x1, waiting for transfers between devices, local(): lax.all_gather(out_weight, 'seq', axis=0, tiled=True)  51.4 us
    all_gather x2, waiting for transfers between devices, prefix(): lax.all_gather(a.astype(kind), axis)  37.4 us
    add x31, other arithmetic, combine_states(): later[0][:, None, None] * earlier[1] + later[1]  35.8 us
    unnamed x55, local copies, waits for them, and re-layouts  34.2 us
    psum x1, waiting for transfers between devices, local(): grad_weight = lax.psum(weight_part, 'dp').astype(jnp.float32) * norm_factor  32.9 us
    dot_general x1, local copies, waits for them, and re-layouts, local(): jnp.dot(columns, lax.all_gather(out_weight, 'seq', axis=0, tiled=True), p...  16.7 us
  transfers between devices with their start and end apart: 5, of which 4 were waited for; matrix products, arithmetic and copies ran while one was open for 20% of the time, Pallas kernels for 0%

commit v1 on v0

--- a/solution.py
+++ b/solution.py
@@ -5,6 +5,11 @@
 
 BLOCK = 128
 EPSILON = 1e-05
+
+
+def gather_over(x, axis, d):
+    sent = jnp.stack([x] * lax.axis_size(axis))
+    return jnp.concatenate(lax.all_to_all(sent, axis, 0, 0), axis=d)
 
 
 def prefix(array, axis, join, neutral, backward):
@@ -163,9 +168,7 @@
     )
     columns = grad_rows
     grad_normed = jnp.dot(
-        columns,
-        lax.all_gather(out_weight, "seq", axis=0, tiled=True),
-        preferred_element_type=jnp.float32,
+        columns, gather_over(out_weight, "seq", 0), preferred_element_type=jnp.float32
     )
     normed = normal.astype(jnp.bfloat16).reshape(tok_count, heads_here * head_dim)
     columns = grad_rows

time: 422 us -> 594 us (1.41)
  blocking collectives: 66.1 us -> 223 us
  waiting for transfers between devices: 201 us -> 163 us
  other arithmetic: 42.3 us -> 75.3 us
  starting transfers between devices: 0.2 us -> 8.99 us
  local copies, waits for them, and re-layouts: 59 us -> 66.9 us
    unnamed x1, blocking collectives: 66.1 us -> 223 us
    all_gather x1 -> x0, waiting for transfers between devices: 51.4 us -> none  [local(): lax.all_gather(out_weight, 'seq', axis=0, tiled=True)]
    all_gather x2, waiting for transfers between devices: 37.4 us -> 81.3 us  [prefix(): lax.all_gather(a.astype(kind), axis)]
    unnamed x6 -> x5, waiting for transfers between devices: 79.8 us -> 50.6 us
    add x31, other arithmetic: 35.8 us -> 64.7 us  [combine_states(): later[0][:, None, None] * earlier[1] + later[1]]
    all_to_all x0 -> x1, starting transfers between devices: none -> 8.65 us  [gather_over(): return jnp.concatenate(lax.all_to_all(sent, axis, 0, 0), axis=d)]
    another operation x2 -> x3, local copies, waits for them, and re-layouts: 0.87 us -> 7.84 us  [the longest x1 6.13 us: gather_over(): sent = jnp.stack([x] * lax.axis_size(axis))]
  transfers between devices with their start and end apart: 5 -> 5, of which waited for: 4 -> 3; matrix products, arithmetic and copies ran while one was open for 20% -> 23% of each run, Pallas kernels for 0% -> 0%
where the time goes in v1:
time: 594 us; the launch traced here: 591 us
  blocking collectives  223 us (38%)
  waiting for transfers between devices  163 us (27%)
  other arithmetic  75.3 us (13%)
  local copies, waits for them, and re-layouts  66.9 us (11%)
  matrix products  36.7 us (6%)
  between operations  17.4 us (3%)
  starting transfers between devices  8.99 us (2%)
    unnamed x1, blocking collectives  223 us
    all_gather x2, waiting for transfers between devices, prefix(): lax.all_gather(a.astype(kind), axis)  81.3 us
    add x31, other arithmetic, combine_states(): later[0][:, None, None] * earlier[1] + later[1]  64.7 us
    unnamed x5, waiting for transfers between devices  50.6 us
    unnamed x55, local copies, waits for them, and re-layouts  35.2 us
    psum x1, waiting for transfers between devices, local(): grad_weight = lax.psum(weight_part, 'dp').astype(jnp.float32) * norm_factor  31.5 us
    dot_general x1, local copies, waits for them, and re-layouts, local(): jnp.dot(columns, gather_over(out_weight, 'seq', 0), preferred_element_typ...  16.7 us
  transfers between devices with their start and end apart: 5, of which 3 were waited for; matrix products, arithmetic and copies ran while one was open for 23% of the time, Pallas kernels for 0%

profile of v1, /device:TPU:1, one launch (start us, length us, event | category | flops | bytes accessed | tf_op | source)
XLA Modules:
  0.0 591.1 jit_solution(8578618005997165564)
XLA Ops:
  13.8 3.3 bitcast_compare_fusion.3
  22.0 2.1 copy.58
  26.7 2.2 convolution_convert_fusion.1
  28.9 6.1 %stack.2 = bf16[32,192,1024]{2,1,0:T(8,128)(2,1)} broadcast(bf16[192,1024]{1,0:T(8,128)(2,1)S(1)} %copy-done.10), dimensions={1,2} | broadcast | bytes 12976128 | tf_op jit(solution)/shard_map/stack | solution.py:11
  35.1 8.6 %all-to-all-start = ((bf16[32,192,1024]{2,1,0:T(8,128)(2,1)}), bf16[32,192,1024]{2,1,0:T(8,128)(2,1)}, u32[]{:S(2)}, u32[]{:S(2)}) async-start(bf16[32,192,1024]{2,1,0:T(8,128)(2,1)} %stack.2), calls=%async_computation | async-start | bytes 25165824 | tf_op jit(solution)/shard_map/all_to_all | solution.py:12
  43.8 2.1 copy.84
  47.7 222.6 %all-reduce.2 = (bf16[256]{0:T(256)(128)(2,1)S(1)}, bf16[256]{0:T(256)(128)(2,1)S(1)}) all-reduce(bf16[256]{0:T(256)(128)(2,1)S(1)} %dynamic-update-slice, bf16[256]{0:T(256)(128)(2,1)S(1)} %dynamic-update-slice.1), channel_id=2, replica_groups=mesh['dp'=2,'seq'=32,'head'=4] {'seq'}, use_global_device_ids=true, to_apply=%add | all-reduce | flops 512 | bytes 2048
  275.0 16.7 %copy.62 = bf16[1024,6144]{1,0:T(8,128)(2,1)} copy(bf16[1024,6144]{0,1:T(8,128)(2,1)} %bitcast.15) | data formatting | bytes 25165824 | tf_op jit(solution)/shard_map/dot_general | solution.py:170
  296.5 6.7 %multiply_reduce_fusion = (f32[256,8]{0,1:T(8,128)S(1)}, f32[256,8,128]{0,2,1:T(8,128)S(1)}) fusion(f32[256,8,128]{0,2,1:T(8,128)S(1)} %get-tuple-element.186, f32[256,8]{0,1:T(8,128)S(1)} %add_rsqrt_fusion, bf16[8,128,6144]{2,1,0:T(8,128)(2,1)} %bitcast.113, bf16[1,256,6144]{2,1,0:T(8,128)(2,1)S(1)} %copy-done), kind=kOutput, calls=%fused_computation.35 | convolution fusion | flops 3222009856 | bytes 17842176 | tf_op jit(solution)/shard_map/dot_general | solution.py:170
  306.2 7.5 %convert_bitcast_fusion = bf16[6144,1024]{0,1:T(8,128)(2,1)} fusion(bf16[256,1024]{0,1:T(8,128)(2,1)} %bitcast.128, bf16[1,256,6144]{2,1,0:T(8,128)(2,1)S(1)} %copy-done), kind=kOutput, calls=%fused_computation.4 | convolution fusion | flops 3227516928 | bytes 16252928 | tf_op jit(solution)/shard_map/dot_general | solution.py:175
  313.7 16.7 %copy.82 = bf16[6144,1024]{1,0:T(8,128)(2,1)} copy(bf16[6144,1024]{0,1:T(8,128)(2,1)} %convert_bitcast_fusion) | data formatting | bytes 25165824
  336.4 2.8 convolution_bitcast_fusion.5
  339.2 2.3 convolution_bitcast_fusion.4
  341.5 81.3 %all-gather.9.cloned.1.call-done = bf16[256,128,128]{2,1,0:T(8,128)(2,1)} async-done(((bf16[8,128,128]{2,1,0:T(8,128)(2,1)}), bf16[256,128,128]{2,1,0:T(8,128)(2,1)}) %all-gather.9.cloned.1.call-update) | async-done | bytes 8388624 | tf_op jit(solution)/shard_map/all_gather | solution.py:20
  423.7 62.9 %while.27 = (s32[]{:T(128)}, f32[8,128,128]{2,1,0:T(8,128)}, s32[]{:T(128)}, bf16[32,8]{1,0:T(8,128)(2,1)S(1)}, bf16[32,8,128,128]{3,2,1,0:T(8,128)(2,1)}, /*index=5*/s32[]{:T(128)}, s32[]{:T(128)}, s32[]{:T(128)}, s32[]{:T(128)}) while((s32[]{:T(128)}, f32[8,128,128]{2,1,0:T(8,128)}, s32[]{:T(128)}, bf16[32,8]{1,0:T(8,128)(2,1)S(1)}, ...), condition=%wide.region_5.6_spmd, body=%wide.region_4.5_spmd.sunk | while | flops 393230 | bytes 1310947 | solution.py:35
  425.8 2.1 convert_add_fusion.5
  427.8 2.1 convert_add_fusion.5
  429.9 2.1 convert_add_fusion.5
  432.0 2.1 convert_add_fusion.5
  434.0 2.1 convert_add_fusion.5
  436.1 2.1 convert_add_fusion.5
  438.2 2.1 convert_add_fusion.5
  440.3 2.1 convert_add_fusion.5
  442.4 2.1 convert_add_fusion.5
  444.6 2.1 convert_add_fusion.5
  446.7 2.1 convert_add_fusion.5
  448.8 2.1 convert_add_fusion.5
  450.9 2.1 convert_add_fusion.5
  453.0 2.1 convert_add_fusion.5
  455.1 2.1 convert_add_fusion.5
  457.3 2.1 convert_add_fusion.5
  459.4 2.1 convert_add_fusion.5
  461.5 2.1 convert_add_fusion.5
  463.7 2.1 convert_add_fusion.5
  465.8 2.1 convert_add_fusion.5
  467.9 2.1 convert_add_fusion.5
  470.0 2.1 convert_add_fusion.5
  472.0 2.1 convert_add_fusion.5
  474.1 2.1 convert_add_fusion.5
  476.2 2.1 convert_add_fusion.5
  482.4 2.1 convert_add_fusion.5
  484.5 2.1 convert_add_fusion.5
  486.6 50.5 %reduce-scatter.4.cloned.1.call-done = bf16[192,1024]{1,0:T(8,128)(2,1)} async-done(((bf16[6144,1024]{1,0:T(8,128)(2,1)}), bf16[192,1024]{1,0:T(8,128)(2,1)}) %reduce-scatter.4.cloned.1.call-update) | async-done | bytes 393232
  539.1 2.7 fusion.13
  543.9 2.7 fusion.12
  548.6 31.5 %all-reduce.5.cloned.1.call-done = bf16[192,1024]{0,1:T(8,128)(2,1)} async-done(((bf16[192,1024]{0,1:T(8,128)(2,1)}), bf16[192,1024]{0,1:T(8,128)(2,1)}) %all-reduce.5.cloned.1.call-update) | async-done | bytes 393232 | tf_op jit(solution)/shard_map/psum | solution.py:185
  580.1 2.1 convert_multiply_fusion
  582.2 2.4 copy.76
  (124 shorter events, 46.5 us)
Async XLA Ops:
  7.2 289.4 %copy-start = (bf16[1,256,6144]{2,1,0:T(8,128)(2,1)S(1)}, bf16[1,256,6144]{2,1,0:T(8,128)(2,1)}, u32[]{:S(2)}) copy-start(bf16[1,256,6144]{2,1,0:T(8,128)(2,1)} %param.14) | copy-start | bytes 9437188
  7.2 17.0 %copy-start.17 = (f32[8]{0:T(128)S(1)}, f32[8]{0:T(128)}, u32[]{:S(2)}) copy-start(f32[8]{0:T(128)} %param.16) | copy-start | bytes 100
  7.2 21.7 %copy-start.10 = (bf16[192,1024]{1,0:T(8,128)(2,1)S(1)}, bf16[192,1024]{1,0:T(8,128)(2,1)}, u32[]{:S(2)}) copy-start(bf16[192,1024]{1,0:T(8,128)(2,1)} %param.15) | copy-start | bytes 1179652
  7.2 284.5 %all-gather.7.cloned.1.call-start = ((), (), s32[]{:S(2)}) async-start(), calls=%async_computation.3 | async-start | bytes 8650752 | tf_op jit(solution)/shard_map/all_gather | solution.py:20
  8.7 0.6 copy-start.13
  24.7 0.5 copy-start.15
  35.0 10.8 %copy-start.20 = (u32[256]{0:T(256)S(1)}, u32[256]{0:T(256)}, u32[]{:S(2)}) copy-start(u32[256]{0:T(256)} %constant.96) | copy-start | bytes 3076
  35.0 12.2 %copy-start.19 = (bf16[8]{0:T(256)(128)(2,1)S(1)}, bf16[8]{0:T(256)(128)(2,1)}, u32[]{:S(2)}) copy-start(bf16[8]{0:T(256)(128)(2,1)} %get-tuple-element.181) | copy-start | bytes 52
  35.0 12.4 %copy-start.18 = (bf16[8]{0:T(256)(128)(2,1)S(1)}, bf16[8]{0:T(256)(128)(2,1)}, u32[]{:S(2)}) copy-start(bf16[8]{0:T(256)(128)(2,1)} %get-tuple-element.180) | copy-start | bytes 52
  35.0 235.3 %copy-start.12 = (f32[256]{0:T(256)S(1)}, f32[256]{0:T(256)}, u32[]{:S(2)}) copy-start(f32[256]{0:T(256)} %iota_convert_fusion) | copy-start | bytes 3076
  35.0 235.3 %copy-start.14 = (s32[256]{0:T(256)S(1)}, s32[256]{0:T(256)}, u32[]{:S(2)}) copy-start(s32[256]{0:T(256)} %copy-done.13) | copy-start | bytes 3076
  35.1 235.6 %copy-start.16 = (f32[8]{0:T(128)S(1)}, f32[8]{0:T(128)}, u32[]{:S(2)}) copy-start(f32[8]{0:T(128)} %copy-done.15) | copy-start | bytes 100
  35.1 239.9 %all-to-all-start = ((bf16[32,192,1024]{2,1,0:T(8,128)(2,1)}), bf16[32,192,1024]{2,1,0:T(8,128)(2,1)}, u32[]{:S(2)}, u32[]{:S(2)}) async-start(bf16[32,192,1024]{2,1,0:T(8,128)(2,1)} %stack.2), calls=%async_computation | async-start | bytes 25165824 | tf_op jit(solution)/shard_map/all_to_all | solution.py:12
  43.7 379.1 %all-gather.9.cloned.1.call-start = ((), (), s32[]{:S(2)}) async-start(), calls=%async_computation.4 | async-start | bytes 8650752 | tf_op jit(solution)/shard_map/all_gather | solution.py:20
  270.4 3.2 copy-start.5
  272.6 1.0 copy-start.6
  303.2 1.9 copy-start.4
  303.2 1.9 copy-start.11
  304.3 0.8 copy-start.2
  306.1 231.0 %reduce-scatter.4.cloned.1.call-start = ((), (), s32[]{:S(2)}) async-start(), calls=%async_computation.5 | async-start | bytes 12976128
  330.4 249.7 %all-reduce.5.cloned.1.call-start = ((), (), s32[]{:S(2)}) async-start(), calls=%async_computation.2 | async-start | bytes 1048576 | tf_op jit(solution)/shard_map/psum | solution.py:185
  330.7 2.0 copy-start.9
  330.7 2.5 copy-start.1
  330.7 2.5 copy-start.3
  332.7 1.6 copy-start.7
  336.4 2.8 copy-start.8
Sparse Core Ops, SparseCore 0:
  29.0 174.9 all-gather.6
  306.3 116.5 all-gather.8
  427.0 110.0 reduce-scatter.3
  539.7 40.3 all-reduce.4
